TPU v7x, 32 devices: a whole 2x2x4 slice. The times are simulated.
32 devices in a mesh: cluster: 16 (over z, x, core), blk: 2 (over y).
Axes of the slice: x: 2, y: 2, z: 4, core: 2. Of those that a mesh axis runs over, the one named last changes fastest.
Arguments:
- coeff: bfloat16 [512, 8, 2048], P('cluster', None, 'blk'), may hold values from -0.375 to 0.375
- intersection: int32 [16, 32], replicated, may hold values from 0 to 511, as said below
- basis_vals: bfloat16 [8192, 256], P(('cluster', 'blk')), may hold values from -6 to 6
- coulomb: bfloat16 [8192, 7, 256], P(('cluster', 'blk')), may hold values from -0.125 to 0.125
- reach: int32 [32], P(('cluster', 'blk')), may hold values from 0 to 3, as said below
Outputs:
- exchange_out: bfloat16 [8192, 2048], P(('cluster', 'blk'))
Inputs may be any that keep to these rules, and one draw needn't show every extreme that they name: `intersection`: each row lists 32 distinct atoms; atom a is owned by cluster a // 32; at most 4 atoms of one row have the same owner, and each row c holds exactly 4 atoms owned by cluster c. `reach`: some block reaches 3 and some block reaches 0.
All inputs are finite; a program needn't handle non-finite values.
Results may differ from a plain program's by a relative error of at most 0.0059.
Values may be sent and summed in bfloat16 or wider, within the bound.
No kernel may reach another device: no remote copies, remote signals or barrier semaphores. Data moves between devices by JAX's collectives and lax.ppermute only.
A program may use at most 64 MiB of HBM per device.

v0:
```python
import jax
import jax.numpy as jnp
from jax import lax
from jax.sharding import PartitionSpec as P


def passed_along(value, axis, steps):
    count = lax.axis_size(axis)
    pairs = [(source, (source + steps) % count) for source in range(count)]
    return lax.ppermute(value, axis, pairs)


def block_term(local_vals, source, coul_tile, within, norm_factor):
    density = (
        lax.dot_general(
            local_vals, source, (((1,), (1,)), ((), ())), preferred_element_type=jnp.float32
        )
        * norm_factor
    )
    masked_tile = jnp.where(
        within, density * coul_tile.astype(jnp.float32), jnp.float32(0.0)
    ).astype(jnp.bfloat16)
    return jnp.dot(masked_tile, source, preferred_element_type=jnp.float32)


def on_device(coeff, intersection, basis_vals, coulomb, reach):
    num_clusters = lax.axis_size("cluster")
    my_cluster = lax.axis_index("cluster")
    atom_count = coeff.shape[0]
    list_len = intersection.shape[1]
    capacity = 2 * list_len // num_clusters
    num_funcs = coeff.shape[1]
    my_columns = coeff.shape[2]
    half_stops = (coulomb.shape[1] - 1) // 2
    owners = intersection // atom_count
    same_owner = owners[:, :, None] == owners[:, None, :]
    earlier = jnp.arange(list_len)[None, :] < jnp.arange(list_len)[:, None]
    slot_rank = jnp.sum(jnp.logical_and(same_owner, earlier[None, :, :]).astype(jnp.int32), axis=2)
    matches = jnp.logical_and(
        (owners == my_cluster)[:, :, None],
        slot_rank[:, :, None] == jnp.arange(capacity)[None, None, :],
    )
    local_atom = intersection - my_cluster * atom_count
    source_rows = jnp.sum(jnp.where(matches, local_atom[:, :, None], 0), axis=1)
    filled = jnp.any(matches, axis=1)
    outgoing = jnp.take(coeff, source_rows.reshape(-1), axis=0)
    outgoing = jnp.where(filled.reshape(-1)[:, None, None], outgoing, jnp.zeros_like(outgoing))
    outgoing = outgoing.reshape(num_clusters, capacity, num_funcs, my_columns)
    incoming = lax.all_to_all(outgoing, "cluster", split_axis=0, concat_axis=0, tiled=True)
    my_owners = lax.dynamic_index_in_dim(owners, my_cluster, 0, keepdims=False)
    my_ranks = lax.dynamic_index_in_dim(slot_rank, my_cluster, 0, keepdims=False)
    positions = my_owners * capacity + my_ranks
    needed = jnp.take(
        incoming.reshape(num_clusters * capacity, num_funcs * my_columns), positions, axis=0
    )
    needed = needed.reshape(list_len * num_funcs, my_columns)
    all_columns = lax.all_gather(needed, "blk", axis=1, tiled=True)

    def convert(values):
        return jnp.dot(values, all_columns, preferred_element_type=jnp.float32).astype(jnp.bfloat16)

    local_vals = convert(basis_vals)
    norm_factor = local_vals.shape[1] ** (-0.5)
    my_reach = reach[0]

    def term(source, offset):
        return block_term(
            local_vals,
            source,
            coulomb[:, offset + half_stops, :],
            abs(offset) <= my_reach,
            norm_factor,
        )

    accumulated = term(local_vals, 0)
    upward = basis_vals
    downward = basis_vals
    for stop_num in range(1, half_stops + 1):
        upward = passed_along(upward, "blk", -1)
        accumulated = accumulated + term(convert(upward), stop_num)
        downward = passed_along(downward, "blk", 1)
        accumulated = accumulated + term(convert(downward), -stop_num)
    return accumulated.astype(jnp.bfloat16)


def solution(mesh):
    return jax.shard_map(
        on_device,
        mesh=mesh,
        in_specs=(
            P("cluster", None, "blk"),
            P(),
            P(("cluster", "blk"), None),
            P(("cluster", "blk"), None, None),
            P(("cluster", "blk")),
        ),
        out_specs=P(("cluster", "blk"), None),
        check_vma=False,
    )
```

profile of v0, /device:TPU:9, one launch (start us, length us, event | category | flops | bytes accessed | tf_op | source)
XLA Modules:
  0.0 91.6 jit_solution(14014058126347180299)
XLA Ops:
  6.5 0.8 broadcast_compare_fusion
  7.3 0.7 broadcast_subtract_fusion
  8.0 0.5 convert_reduce_fusion
  8.7 0.2 fusion.54
  9.2 0.6 gather_fusion
  9.8 1.2 %select_select_fusion = bf16[16,4,8,1024]{3,2,1,0:T(8,128)(2,1)} fusion(bf16[16,4,8,1024]{3,2,1,0:T(8,128)(2,1)S(1)} %bitcast.82, pred[16,4]{1,0:T(8,128)(4,1)S(1)} %copy.7, pred[16,4]{1,0:T(8,128)(4,1)S(1)} %copy.6), kind=kLoop, calls=%fused_computation.21 | loop fusion | flops 1048576 | bytes 2097280 | tf_op jit(solution)/shard_map/jit(_where)/select_n | solution.py:47
  11.0 6.5 %all-to-all-start = ((bf16[16,4,8,1024]{3,2,1,0:T(8,128)(2,1)}), bf16[16,4,8,1024]{3,2,1,0:T(8,128)(2,1)S(1)}, u32[]{:S(2)}, u32[]{:S(2)}) async-start(bf16[16,4,8,1024]{3,2,1,0:T(8,128)(2,1)} %select_select_fusion), calls=%async_computation | async-start | bytes 2097152 | tf_op jit(solution)/shard_map/all_to_all | solution.py:49
  17.8 24.7 %all-to-all-done = bf16[16,4,8,1024]{3,2,1,0:T(8,128)(2,1)S(1)} async-done(((bf16[16,4,8,1024]{3,2,1,0:T(8,128)(2,1)}), bf16[16,4,8,1024]{3,2,1,0:T(8,128)(2,1)S(1)}, u32[]{:S(2)}, u32[]{:S(2)}) %all-to-all-start) | async-done | bytes 1048608 | tf_op jit(solution)/shard_map/all_to_all | solution.py:49
  42.5 0.6 copy.9
  43.1 0.9 gather_fusion.1
  44.0 0.2 gather.15
  44.2 0.9 broadcast_select_fusion
  45.2 1.3 %collective-permute-start = (bf16[256,256]{1,0:T(8,128)(2,1)S(1)}, bf16[256,256]{1,0:T(8,128)(2,1)S(1)}, u32[]{:S(2)}, u32[]{:S(2)}) collective-permute-start(bf16[256,256]{1,0:T(8,128)(2,1)S(1)} %copy-done.5), channel_id=1, source_target_pairs={{0,1},{1,0},{2,3},{3,2},{4,5},{5,4},{6,7},{7,6},{8,9},{9,8},{10,11... | collective-permute-start | bytes 393224 | tf_op jit(solution)/shard_map/ppermute | solution.py:10
  46.5 4.3 %collective-permute-done = bf16[256,256]{1,0:T(8,128)(2,1)S(1)} collective-permute-done((bf16[256,256]{1,0:T(8,128)(2,1)S(1)}, bf16[256,256]{1,0:T(8,128)(2,1)S(1)}, u32[]{:S(2)}, u32[]{:S(2)}) %collective-permute-start) | collective-permute-done | bytes 131104 | tf_op jit(solution)/shard_map/ppermute | solution.py:10
  50.7 1.2 %collective-permute-start.1 = (bf16[256,256]{1,0:T(8,128)(2,1)S(1)}, bf16[256,256]{1,0:T(8,128)(2,1)S(1)}, u32[]{:S(2)}, u32[]{:S(2)}) collective-permute-start(bf16[256,256]{1,0:T(8,128)(2,1)S(1)} %collective-permute-done), channel_id=1, source_target_pairs={{0,1},{1,0},{2,3},{3,2},{4,5},{5,4},{6,7},{7,6},{8,9},{9,8},{10,11... | collective-permute-start | bytes 393224 | tf_op jit(solution)/shard_map/ppermute | solution.py:10
  52.7 4.1 %collective-permute-done.1 = bf16[256,256]{1,0:T(8,128)(2,1)S(1)} collective-permute-done((bf16[256,256]{1,0:T(8,128)(2,1)S(1)}, bf16[256,256]{1,0:T(8,128)(2,1)S(1)}, u32[]{:S(2)}, u32[]{:S(2)}) %collective-permute-start.1) | collective-permute-done | bytes 131104 | tf_op jit(solution)/shard_map/ppermute | solution.py:10
  56.7 2.3 %collective-permute-start.2 = (bf16[256,256]{1,0:T(8,128)(2,1)S(1)}, bf16[256,256]{1,0:T(8,128)(2,1)S(1)}, u32[]{:S(2)}, u32[]{:S(2)}) collective-permute-start(bf16[256,256]{1,0:T(8,128)(2,1)S(1)} %collective-permute-done.1), channel_id=1, source_target_pairs={{0,1},{1,0},{2,3},{3,2},{4,5},{5,4},{6,7},{7,6},{8,9},{9,8},{10,11... | collective-permute-start | bytes 393224 | tf_op jit(solution)/shard_map/ppermute | solution.py:10
  59.0 11.4 %all-gather.2.cloned.1.call-done = bf16[256,2048]{1,0:T(8,128)(2,1)} async-done(((bf16[256,1024]{1,0:T(8,128)(2,1)}), bf16[256,2048]{1,0:T(8,128)(2,1)}) %all-gather.2.cloned.1.call-update) | async-done | bytes 1048592 | tf_op jit(solution)/shard_map/all_gather | solution.py:57
  70.4 1.8 %convolution_convert_fusion.2 = bf16[2048,256]{1,0:T(8,128)(2,1)S(1)} fusion(bf16[256,2048]{1,0:T(8,128)(2,1)} %all-gather.2.cloned.1.call-done, bf16[256,256]{1,0:T(8,128)(2,1)S(1)} %collective-permute-done), kind=kOutput, calls=%fused_computation.11 | convolution fusion | flops 268959744 | bytes 2228224 | tf_op jit(solution)/shard_map/dot_general | solution.py:60
  72.2 0.5 convolution_convert_fusion.3
  72.7 0.5 convolution_multiply_fusion.2
  73.2 3.6 %fusion.4 = f32[256,2048]{1,0:T(8,128)} fusion(bf16[2048,256]{1,0:T(8,128)(2,1)S(1)} %convolution_convert_fusion.3, bf16[256,7,256]{2,0,1:T(8,128)(2,1)} %param.8, pred[]{:T(512)} %bitcast), kind=kOutput, calls=%fused_computation.20 | convolution fusion | flops 537198592 | bytes 5374464 | tf_op jit(solution)/shard_map/dot_general | solution.py:23
  76.8 2.6 %convolution_add_fusion.5 = f32[256,2048]{1,0:T(8,128)S(1)} fusion(f32[256,2048]{1,0:T(8,128)} %fusion.4, bf16[2048,256]{1,0:T(8,128)(2,1)} %copy-done.2, f32[256,256]{1,0:T(8,128)S(1)} %convolution_multiply_fusion.2, bf16[256,7,256]{2,0,1:T(8,128)(2,1)} %param.8, pred[]{:T(512)} %bitcast.7), kind=kOutput, calls=%fused_computation.7 | convolution fusion | flops 269221888 | bytes 5636608 | tf_op jit(solution)/shard_map/dot_general | solution.py:23
  79.4 0.5 convolution_add_fusion.4
  79.8 0.5 convolution_convert_fusion.1
  80.3 0.5 convolution_multiply_fusion.1
  80.8 0.5 convolution_add_fusion.3
  81.3 0.5 convolution_add_fusion.2
  81.8 0.5 convolution_convert_fusion
  82.3 0.5 convolution_multiply_fusion
  82.8 0.5 convolution_add_fusion.1
  83.3 1.4 %fusion = bf16[256,2048]{1,0:T(8,128)(2,1)} fusion(f32[256,2048]{1,0:T(8,128)S(1)} %convolution_add_fusion.1, bf16[2048,256]{1,0:T(8,128)(2,1)S(1)} %convolution_convert_fusion, f32[256,256]{1,0:T(8,128)S(1)} %convolution_multiply_fusion, bf16[256,7,256]{2,0,1:T(8,128)(2,1)S(1)} %copy-done.4, pred[]{:T(512)} %bitcast.13), kind=kOutput, calls=%fused_computation.8 | convolution fusion | flops 269746176 | bytes 4587521 | tf_op jit(solution)/shard_map/dot_general | solution.py:23
  (29 shorter events, 0.8 us)
Async XLA Ops:
  6.5 2.7 %copy-start = (bf16[32,8,1024]{2,1,0:T(8,128)(2,1)S(1)}, bf16[32,8,1024]{2,1,0:T(8,128)(2,1)}, u32[]{:S(2)}) copy-start(bf16[32,8,1024]{2,1,0:T(8,128)(2,1)} %param.5) | copy-start | bytes 1572868
  11.0 31.5 %all-to-all-start = ((bf16[16,4,8,1024]{3,2,1,0:T(8,128)(2,1)}), bf16[16,4,8,1024]{3,2,1,0:T(8,128)(2,1)S(1)}, u32[]{:S(2)}, u32[]{:S(2)}) async-start(bf16[16,4,8,1024]{3,2,1,0:T(8,128)(2,1)} %select_select_fusion), calls=%async_computation | async-start | bytes 2097152 | tf_op jit(solution)/shard_map/all_to_all | solution.py:49
  17.6 52.8 %all-gather.2.cloned.1.call-start = ((), (), s32[]{:S(2)}) async-start(), calls=%async_computation.1 | async-start | bytes 1572864 | tf_op jit(solution)/shard_map/all_gather | solution.py:57
  44.0 1.2 %copy-start.5 = (bf16[256,256]{1,0:T(8,128)(2,1)S(1)}, bf16[256,256]{1,0:T(8,128)(2,1)}, u32[]{:S(2)}) copy-start(bf16[256,256]{1,0:T(8,128)(2,1)} %param.7) | copy-start | bytes 393220
  45.2 5.6 %collective-permute-start = (bf16[256,256]{1,0:T(8,128)(2,1)S(1)}, bf16[256,256]{1,0:T(8,128)(2,1)S(1)}, u32[]{:S(2)}, u32[]{:S(2)}) collective-permute-start(bf16[256,256]{1,0:T(8,128)(2,1)S(1)} %copy-done.5), channel_id=1, source_target_pairs={{0,1},{1,0},{2,3},{3,2},{4,5},{5,4},{6,7},{7,6},{8,9},{9,8},{10,11... | collective-permute-start | bytes 393224 | tf_op jit(solution)/shard_map/ppermute | solution.py:10
  50.7 6.0 %collective-permute-start.1 = (bf16[256,256]{1,0:T(8,128)(2,1)S(1)}, bf16[256,256]{1,0:T(8,128)(2,1)S(1)}, u32[]{:S(2)}, u32[]{:S(2)}) collective-permute-start(bf16[256,256]{1,0:T(8,128)(2,1)S(1)} %collective-permute-done), channel_id=1, source_target_pairs={{0,1},{1,0},{2,3},{3,2},{4,5},{5,4},{6,7},{7,6},{8,9},{9,8},{10,11... | collective-permute-start | bytes 393224 | tf_op jit(solution)/shard_map/ppermute | solution.py:10
  56.7 25.1 %collective-permute-start.2 = (bf16[256,256]{1,0:T(8,128)(2,1)S(1)}, bf16[256,256]{1,0:T(8,128)(2,1)S(1)}, u32[]{:S(2)}, u32[]{:S(2)}) collective-permute-start(bf16[256,256]{1,0:T(8,128)(2,1)S(1)} %collective-permute-done.1), channel_id=1, source_target_pairs={{0,1},{1,0},{2,3},{3,2},{4,5},{5,4},{6,7},{7,6},{8,9},{9,8},{10,11... | collective-permute-start | bytes 393224 | tf_op jit(solution)/shard_map/ppermute | solution.py:10
  70.4 1.8 %copy-start.1 = (bf16[256,2048]{1,0:T(8,128)(2,1)S(1)}, bf16[256,2048]{1,0:T(8,128)(2,1)}, u32[]{:S(2)}) copy-start(bf16[256,2048]{1,0:T(8,128)(2,1)} %all-gather.2.cloned.1.call-done) | copy-start | bytes 3145732
  72.2 1.0 %copy-start.2 = (bf16[2048,256]{1,0:T(8,128)(2,1)}, bf16[2048,256]{1,0:T(8,128)(2,1)S(1)}, u32[]{:S(2)}) copy-start(bf16[2048,256]{1,0:T(8,128)(2,1)S(1)} %convolution_convert_fusion.2) | copy-start | bytes 3145732
  76.8 2.6 %copy-start.3 = (bf16[2048,256]{1,0:T(8,128)(2,1)S(1)}, bf16[2048,256]{1,0:T(8,128)(2,1)}, u32[]{:S(2)}) copy-start(bf16[2048,256]{1,0:T(8,128)(2,1)} %copy-done.2) | copy-start | bytes 3145732
  76.8 2.6 %copy-start.4 = (bf16[256,7,256]{2,0,1:T(8,128)(2,1)S(1)}, bf16[256,7,256]{2,0,1:T(8,128)(2,1)}, u32[]{:S(2)}) copy-start(bf16[256,7,256]{2,0,1:T(8,128)(2,1)} %param.8) | copy-start | bytes 2752516
Sparse Core Ops, SparseCore 0:
  45.3 25.0 all-gather.1
where the time goes:
time: 91.9 us; the launch traced here: 91.6 us
  waiting for transfers between devices  44.4 us (48%)
  between operations  14.3 us (16%)
  matrix products  14.2 us (15%)
  starting transfers between devices  11.4 us (12%)
  other arithmetic  4.38 us (5%)
  local copies, waits for them, and re-layouts  2.91 us (3%)
    all_to_all x1, waiting for transfers between devices, on_device(): lax.all_to_all(outgoing, 'cluster', split_axis=0, concat_axis=0, tiled=True)  24.7 us
    all_gather x1, waiting for transfers between devices, on_device(): all_columns = lax.all_gather(needed, 'blk', axis=1, tiled=True)  11.4 us
    dot_general x7, matrix products, block_term(): return jnp.dot(masked_tile, source, preferred_element_type=jnp.float32)  9.46 us
    ppermute x3, waiting for transfers between devices, passed_along(): return lax.ppermute(value, axis, pairs)  8.35 us
    all_to_all x1, starting transfers between devices, on_device(): lax.all_to_all(outgoing, 'cluster', split_axis=0, concat_axis=0, tiled=True)  6.55 us
    ppermute x3, starting transfers between devices, passed_along(): return lax.ppermute(value, axis, pairs)  4.85 us
    dot_general x4, matrix products, convert(): jnp.dot(values, all_columns, preferred_element_type=jnp.float32)  3.26 us
  transfers between devices with their start and end apart: 5, of which 4 were waited for; matrix products, arithmetic and copies ran while one was open for 13% of the time, Pallas kernels for 0%

commit v1 on v0

--- a/solution.py
+++ b/solution.py
@@ -2,6 +2,28 @@
 import jax.numpy as jnp
 from jax import lax
 from jax.sharding import PartitionSpec as P
+
+
+def in_order(pieces, dim):
+    shape = list(pieces.shape[1:])
+    shape[dim] *= pieces.shape[0]
+    return jnp.moveaxis(pieces, 0, dim).reshape(shape)
+
+
+def collected_by_bits(value, axis):
+    size = lax.axis_size(axis)
+    blocks = value[None]
+    for level in range(size.bit_length() - 1):
+        stride = 1 << level
+        theirs = lax.ppermute(blocks, axis, [(i, i ^ stride) for i in range(size)])
+        both = jnp.stack([blocks, theirs])
+        upper = lax.axis_index(axis) >> level & 1
+        blocks = jnp.where(upper == 0, both, both[::-1]).reshape(-1, *value.shape)
+    return blocks
+
+
+def collect(x, axis, dim):
+    return in_order(collected_by_bits(x, axis), dim)
 
 
 def passed_along(value, axis, steps):
@@ -54,7 +76,7 @@
         incoming.reshape(num_clusters * capacity, num_funcs * my_columns), positions, axis=0
     )
     needed = needed.reshape(list_len * num_funcs, my_columns)
-    all_columns = lax.all_gather(needed, "blk", axis=1, tiled=True)
+    all_columns = collect(needed, "blk", 1)
 
     def convert(values):
         return jnp.dot(values, all_columns, preferred_element_type=jnp.float32).astype(jnp.bfloat16)

time: 91.9 us -> 76.5 us (0.83)
  between operations: 14.3 us -> 0.92 us
  waiting for transfers between devices: 44.4 us -> 42.7 us
  local copies, waits for them, and re-layouts: 2.91 us -> 4.51 us
  matrix products: 14.2 us -> 12.7 us
    all_gather x1 -> x0, waiting for transfers between devices: 11.4 us -> none  [on_device(): all_columns = lax.all_gather(needed, 'blk', axis=1, tiled=True)]
    ppermute x3, waiting for transfers between devices: 8.35 us -> 18 us  [passed_along(): return lax.ppermute(value, axis, pairs)]
    ppermute x3, starting transfers between devices: 4.85 us -> 2.79 us  [passed_along(): return lax.ppermute(value, axis, pairs)]
    dot_general x4, matrix products: 3.26 us -> 1.85 us  [convert(): jnp.dot(values, all_columns, preferred_element_type=jnp.float32)]
    ppermute x0 -> x1, starting transfers between devices: none -> 1.3 us  [collected_by_bits(): theirs = lax.ppermute(blocks, axis, [(i, i ^ stride) for i in range(size)])]
    unnamed x13 -> x11, local copies, waits for them, and re-layouts: 0.63 us -> 1.58 us
  transfers between devices with their start and end apart: 5 -> 5, of which waited for: 4 -> 3; matrix products, arithmetic and copies ran while one was open for 13% -> 14% of each run, Pallas kernels for 0% -> 0%
where the time goes in v1:
time: 76.5 us; the launch traced here: 75.3 us
  waiting for transfers between devices  42.7 us (56%)
  matrix products  12.7 us (17%)
  starting transfers between devices  10.6 us (14%)
  local copies, waits for them, and re-layouts  4.51 us (6%)
  other arithmetic  3.86 us (5%)
  between operations  0.92 us (1%)
    all_to_all x1, waiting for transfers between devices, on_device(): lax.all_to_all(outgoing, 'cluster', split_axis=0, concat_axis=0, tiled=True)  24.7 us
    ppermute x3, waiting for transfers between devices, passed_along(): return lax.ppermute(value, axis, pairs)  18 us
    dot_general x7, matrix products, block_term(): return jnp.dot(masked_tile, source, preferred_element_type=jnp.float32)  9.44 us
    all_to_all x1, starting transfers between devices, on_device(): lax.all_to_all(outgoing, 'cluster', split_axis=0, concat_axis=0, tiled=True)  6.55 us
    ppermute x3, starting transfers between devices, passed_along(): return lax.ppermute(value, axis, pairs)  2.79 us
    dot_general x4, matrix products, convert(): jnp.dot(values, all_columns, preferred_element_type=jnp.float32)  1.85 us
    gather x5, local copies, waits for them, and re-layouts, on_device(): jnp.take(incoming.reshape(num_clusters * capacity, num_funcs * my_columns...  1.77 us
    unnamed x11, local copies, waits for them, and re-layouts  1.58 us
  transfers between devices with their start and end apart: 5, of which 3 were waited for; matrix products, arithmetic and copies ran while one was open for 14% of the time, Pallas kernels for 0%

profile of v1, /device:TPU:9, one launch (start us, length us, event | category | flops | bytes accessed | tf_op | source)
XLA Modules:
  0.0 75.3 jit_solution(730649786990359814)
XLA Ops:
  0.0 0.8 %broadcast_compare_fusion = (pred[16,32]{1,0:T(8,128)(4,1)S(1)}, s32[16,32]{1,0:T(8,128)S(1)}) fusion(s32[]{:T(128)S(6)} %axis_index.25, s32[16,32]{1,0:T(8,128)} %param.6), kind=kLoop, calls=%fused_computation.91 | loop fusion | flops 8192 | bytes 4612 | tf_op jit(solution)/shard_map/eq | solution.py:62
  0.8 0.7 broadcast_subtract_fusion
  1.5 0.5 convert_reduce_fusion
  2.7 0.6 gather_fusion
  3.3 1.2 %select_select_fusion = bf16[16,4,8,1024]{3,2,1,0:T(8,128)(2,1)} fusion(bf16[16,4,8,1024]{3,2,1,0:T(8,128)(2,1)S(1)} %bitcast.92, pred[16,4]{1,0:T(8,128)(4,1)S(1)} %copy.9, pred[16,4]{1,0:T(8,128)(4,1)S(1)} %copy.8), kind=kLoop, calls=%fused_computation.23 | loop fusion | flops 1048576 | bytes 2097280 | tf_op jit(solution)/shard_map/jit(_where)/select_n | solution.py:69
  4.5 6.5 %all-to-all-start = ((bf16[16,4,8,1024]{3,2,1,0:T(8,128)(2,1)}), bf16[16,4,8,1024]{3,2,1,0:T(8,128)(2,1)S(1)}, u32[]{:S(2)}, u32[]{:S(2)}) async-start(bf16[16,4,8,1024]{3,2,1,0:T(8,128)(2,1)} %select_select_fusion), calls=%async_computation | async-start | bytes 2097152 | tf_op jit(solution)/shard_map/all_to_all | solution.py:71
  11.2 24.7 %all-to-all-done = bf16[16,4,8,1024]{3,2,1,0:T(8,128)(2,1)S(1)} async-done(((bf16[16,4,8,1024]{3,2,1,0:T(8,128)(2,1)}), bf16[16,4,8,1024]{3,2,1,0:T(8,128)(2,1)S(1)}, u32[]{:S(2)}, u32[]{:S(2)}) %all-to-all-start) | async-done | bytes 1048608 | tf_op jit(solution)/shard_map/all_to_all | solution.py:71
  35.9 0.6 copy.13
  36.5 0.9 %gather_fusion.1 = bf16[32,8192]{1,0:T(8,128)(2,1)S(1)} fusion(bf16[64,8192]{1,0:T(8,128)(2,1)S(1)} %bitcast.91, s32[1024]{0:T(1024)S(1)} %pad_clamp_fusion), kind=kCustom, calls=%fused_computation.1 | custom fusion | bytes 1048704 | tf_op jit(solution)/shard_map/jit(_take)/gather | solution.py:75
  37.4 0.2 gather.18
  38.0 1.3 %collective-permute-start = (bf16[1,256,1024]{1,2,0:T(8,128)(2,1)S(1)}, bf16[1,256,1024]{1,2,0:T(8,128)(2,1)S(1)}, u32[]{:S(2)}, u32[]{:S(2)}) collective-permute-start(bf16[1,256,1024]{1,2,0:T(8,128)(2,1)S(1)} %broadcast_select_fusion), channel_id=1, source_target_pairs={{0,1},{1,0},{2,3},{3,2},{4,5},{5,4},{6,7},{7,6},{8,9},{9,8},{10,11... | collective-permute-start | bytes 1572872 | tf_op jit(solution)/shard_map/ppermute | solution.py:18
  39.3 0.3 collective-permute-start.1
  39.6 15.2 %collective-permute-done.1 = bf16[256,256]{1,0:T(8,128)(2,1)S(1)} collective-permute-done((bf16[256,256]{1,0:T(8,128)(2,1)S(1)}, bf16[256,256]{1,0:T(8,128)(2,1)S(1)}, u32[]{:S(2)}, u32[]{:S(2)}) %collective-permute-start.1) | collective-permute-done | bytes 131104 | tf_op jit(solution)/shard_map/ppermute | solution.py:32
  54.8 1.2 %collective-permute-start.2 = (bf16[256,256]{1,0:T(8,128)(2,1)S(1)}, bf16[256,256]{1,0:T(8,128)(2,1)S(1)}, u32[]{:S(2)}, u32[]{:S(2)}) collective-permute-start(bf16[256,256]{1,0:T(8,128)(2,1)S(1)} %collective-permute-done.1), channel_id=1, source_target_pairs={{0,1},{1,0},{2,3},{3,2},{4,5},{5,4},{6,7},{7,6},{8,9},{9,8},{10,11... | collective-permute-start | bytes 393224 | tf_op jit(solution)/shard_map/ppermute | solution.py:32
  56.7 2.8 %collective-permute-done.2 = bf16[256,256]{1,0:T(8,128)(2,1)S(1)} collective-permute-done((bf16[256,256]{1,0:T(8,128)(2,1)S(1)}, bf16[256,256]{1,0:T(8,128)(2,1)S(1)}, u32[]{:S(2)}, u32[]{:S(2)}) %collective-permute-start.2) | collective-permute-done | bytes 131104 | tf_op jit(solution)/shard_map/ppermute | solution.py:32
  59.4 1.2 %collective-permute-start.3 = (bf16[256,256]{1,0:T(8,128)(2,1)S(1)}, bf16[256,256]{1,0:T(8,128)(2,1)S(1)}, u32[]{:S(2)}, u32[]{:S(2)}) collective-permute-start(bf16[256,256]{1,0:T(8,128)(2,1)S(1)} %collective-permute-done.2), channel_id=1, source_target_pairs={{0,1},{1,0},{2,3},{3,2},{4,5},{5,4},{6,7},{7,6},{8,9},{9,8},{10,11... | collective-permute-start | bytes 393224 | tf_op jit(solution)/shard_map/ppermute | solution.py:32
  60.7 0.2 gather.17
  61.5 0.5 convolution_convert_fusion.3
  62.0 0.5 convolution_convert_fusion.2
  62.5 1.0 %copy-done.1 = bf16[2048,256]{1,0:T(8,128)(2,1)} copy-done((bf16[2048,256]{1,0:T(8,128)(2,1)}, bf16[2048,256]{1,0:T(8,128)(2,1)S(1)}, u32[]{:S(2)}) %copy-start.1) | copy-done | bytes 1048600
  63.4 0.5 convolution_multiply_fusion.2
  63.9 3.5 %fusion.4 = f32[256,2048]{1,0:T(8,128)} fusion(bf16[2048,256]{1,0:T(8,128)(2,1)S(1)} %convolution_convert_fusion.3, bf16[256,7,256]{2,0,1:T(8,128)(2,1)} %param.8, pred[]{:T(512)} %bitcast), kind=kOutput, calls=%fused_computation.21 | convolution fusion | flops 537198592 | bytes 5374464 | tf_op jit(solution)/shard_map/dot_general | solution.py:45
  67.4 2.6 %convolution_add_fusion.5 = f32[256,2048]{1,0:T(8,128)S(1)} fusion(f32[256,2048]{1,0:T(8,128)} %fusion.4, bf16[2048,256]{1,0:T(8,128)(2,1)} %copy-done.1, f32[256,256]{1,0:T(8,128)S(1)} %convolution_multiply_fusion.2, bf16[256,7,256]{2,0,1:T(8,128)(2,1)} %param.8, pred[]{:T(512)} %bitcast.11), kind=kOutput, calls=%fused_computation.7 | convolution fusion | flops 269221888 | bytes 5636608 | tf_op jit(solution)/shard_map/dot_general | solution.py:45
  70.0 0.5 convolution_add_fusion.4
  70.5 0.5 convolution_convert_fusion.1
  71.0 0.5 convolution_multiply_fusion.1
  71.5 0.5 convolution_add_fusion.3
  71.9 0.5 convolution_add_fusion.2
  72.4 0.5 convolution_convert_fusion
  72.9 0.5 convolution_multiply_fusion
  73.4 0.5 convolution_add_fusion.1
  73.9 1.4 %fusion = bf16[256,2048]{1,0:T(8,128)(2,1)} fusion(f32[256,2048]{1,0:T(8,128)S(1)} %convolution_add_fusion.1, bf16[2048,256]{1,0:T(8,128)(2,1)S(1)} %convolution_convert_fusion, f32[256,256]{1,0:T(8,128)S(1)} %convolution_multiply_fusion, bf16[256,7,256]{2,0,1:T(8,128)(2,1)S(1)} %copy-done.3, pred[]{:T(512)} %bitcast.19), kind=kOutput, calls=%fused_computation.8 | convolution fusion | flops 269746176 | bytes 4587521 | tf_op jit(solution)/shard_map/dot_general | solution.py:45
  (32 shorter events, 1.7 us)
Async XLA Ops:
  0.0 2.7 %copy-start = (bf16[32,8,1024]{2,1,0:T(8,128)(2,1)S(1)}, bf16[32,8,1024]{2,1,0:T(8,128)(2,1)}, u32[]{:S(2)}) copy-start(bf16[32,8,1024]{2,1,0:T(8,128)(2,1)} %param.5) | copy-start | bytes 1572868
  4.5 31.5 %all-to-all-start = ((bf16[16,4,8,1024]{3,2,1,0:T(8,128)(2,1)}), bf16[16,4,8,1024]{3,2,1,0:T(8,128)(2,1)S(1)}, u32[]{:S(2)}, u32[]{:S(2)}) async-start(bf16[16,4,8,1024]{3,2,1,0:T(8,128)(2,1)} %select_select_fusion), calls=%async_computation | async-start | bytes 2097152 | tf_op jit(solution)/shard_map/all_to_all | solution.py:71
  37.4 1.8 %copy-start.4 = (bf16[256,256]{1,0:T(8,128)(2,1)S(1)}, bf16[256,256]{1,0:T(8,128)(2,1)}, u32[]{:S(2)}) copy-start(bf16[256,256]{1,0:T(8,128)(2,1)} %param.7) | copy-start | bytes 393220
  38.0 23.2 %collective-permute-start = (bf16[1,256,1024]{1,2,0:T(8,128)(2,1)S(1)}, bf16[1,256,1024]{1,2,0:T(8,128)(2,1)S(1)}, u32[]{:S(2)}, u32[]{:S(2)}) collective-permute-start(bf16[1,256,1024]{1,2,0:T(8,128)(2,1)S(1)} %broadcast_select_fusion), channel_id=1, source_target_pairs={{0,1},{1,0},{2,3},{3,2},{4,5},{5,4},{6,7},{7,6},{8,9},{9,8},{10,11... | collective-permute-start | bytes 1572872 | tf_op jit(solution)/shard_map/ppermute | solution.py:18
  39.3 15.5 %collective-permute-start.1 = (bf16[256,256]{1,0:T(8,128)(2,1)S(1)}, bf16[256,256]{1,0:T(8,128)(2,1)S(1)}, u32[]{:S(2)}, u32[]{:S(2)}) collective-permute-start(bf16[256,256]{1,0:T(8,128)(2,1)S(1)} %copy-done.4), channel_id=1, source_target_pairs={{0,1},{1,0},{2,3},{3,2},{4,5},{5,4},{6,7},{7,6},{8,9},{9,8},{10,11... | collective-permute-start | bytes 393224 | tf_op jit(solution)/shard_map/ppermute | solution.py:32
  54.8 4.7 %collective-permute-start.2 = (bf16[256,256]{1,0:T(8,128)(2,1)S(1)}, bf16[256,256]{1,0:T(8,128)(2,1)S(1)}, u32[]{:S(2)}, u32[]{:S(2)}) collective-permute-start(bf16[256,256]{1,0:T(8,128)(2,1)S(1)} %collective-permute-done.1), channel_id=1, source_target_pairs={{0,1},{1,0},{2,3},{3,2},{4,5},{5,4},{6,7},{7,6},{8,9},{9,8},{10,11... | collective-permute-start | bytes 393224 | tf_op jit(solution)/shard_map/ppermute | solution.py:32
  59.4 13.0 %collective-permute-start.3 = (bf16[256,256]{1,0:T(8,128)(2,1)S(1)}, bf16[256,256]{1,0:T(8,128)(2,1)S(1)}, u32[]{:S(2)}, u32[]{:S(2)}) collective-permute-start(bf16[256,256]{1,0:T(8,128)(2,1)S(1)} %collective-permute-done.2), channel_id=1, source_target_pairs={{0,1},{1,0},{2,3},{3,2},{4,5},{5,4},{6,7},{7,6},{8,9},{9,8},{10,11... | collective-permute-start | bytes 393224 | tf_op jit(solution)/shard_map/ppermute | solution.py:32
  62.4 1.0 %copy-start.1 = (bf16[2048,256]{1,0:T(8,128)(2,1)}, bf16[2048,256]{1,0:T(8,128)(2,1)S(1)}, u32[]{:S(2)}) copy-start(bf16[2048,256]{1,0:T(8,128)(2,1)S(1)} %convolution_convert_fusion.2) | copy-start | bytes 3145732
  67.4 2.6 %copy-start.2 = (bf16[2048,256]{1,0:T(8,128)(2,1)S(1)}, bf16[2048,256]{1,0:T(8,128)(2,1)}, u32[]{:S(2)}) copy-start(bf16[2048,256]{1,0:T(8,128)(2,1)} %copy-done.1) | copy-start | bytes 3145732
  67.4 2.6 %copy-start.3 = (bf16[256,7,256]{2,0,1:T(8,128)(2,1)S(1)}, bf16[256,7,256]{2,0,1:T(8,128)(2,1)}, u32[]{:S(2)}) copy-start(bf16[256,7,256]{2,0,1:T(8,128)(2,1)} %param.8) | copy-start | bytes 2752516
